TPU v7x, 256 devices: a whole 4x4x8 slice. The times are simulated.
256 devices in a mesh: dp: 32 (over x, z), expert: 8 (over y, core).
Axes of the slice: x: 4, y: 4, z: 8, core: 2. Of those that a mesh axis runs over, the one named last changes fastest.
Arguments:
- tokens: bfloat16 [4096, 4096], P('dp', 'expert'), may hold values from -6 to 6
- expert_ids: int32 [4096, 8], P('dp'), may hold values from 0 to 31, all different within a row; in each aligned block of 128 rows (0 to 127, 128 to 255, ...) at most 40 rows name the same one
- scores: float32 [4096, 8], P('dp'), may hold values from 0.05 to 1
- weight_in: bfloat16 [32, 4096, 2048], P('dp', 'expert'), may hold values from -0.09375 to 0.09375
- weight_out: bfloat16 [32, 1024, 4096], P('dp', None, 'expert'), may hold values from -0.1875 to 0.1875
- out_grad: bfloat16 [4096, 4096], P('dp', 'expert'), may hold values from -6 to 6
Outputs:
- layer_out: bfloat16 [4096, 4096], P('dp', 'expert')
- tokens_grad: bfloat16 [4096, 4096], P('dp', 'expert')
- scores_grad: float32 [4096, 8], P('dp')
- w_in_grad: bfloat16 [32, 4096, 2048], P('dp', 'expert')
- w_out_grad: bfloat16 [32, 1024, 4096], P('dp', None, 'expert')
Inputs may be any that keep to these rules, and one draw needn't show every extreme that they name: `expert_ids`: the 8 experts of a token differ. Among the 128 consecutive tokens of one index of dp no expert is named by more than 40 choices, and in every draw some such block names some expert exactly 40 times.
All inputs are finite; a program needn't handle non-finite values.
Results may differ from a plain program's by a relative error of at most 0.0064.
Values may be sent and summed in bfloat16 or wider, within the bound.
No kernel may reach another device: no remote copies, remote signals or barrier semaphores. Data moves between devices by JAX's collectives and lax.ppermute only.
A program may use at most 128 MiB of HBM per device.

v0:
```python
import jax
import jax.numpy as jnp
from jax import lax
from jax.sharding import PartitionSpec as P

ROUTE_SCALE = 2.5


def gate_terms(gate_up, hidden_units):
    gate = gate_up[:, :hidden_units]
    upward = gate_up[:, hidden_units:]
    return (gate, upward, jax.nn.sigmoid(gate))


def gate_backward(hidden_grad, gate, upward, sigma):
    return jnp.concatenate(
        [hidden_grad * upward * sigma * (1.0 + gate * (1.0 - sigma)), hidden_grad * gate * sigma],
        axis=1,
    ).astype(jnp.bfloat16)


def body(tokens, expert_ids, scores, weight_in, weight_out, out_grad):
    n_data = lax.axis_size("dp")
    tok_count, slab_width = tokens.shape
    top_count = expert_ids.shape[1]
    hidden_units = weight_out.shape[1]
    capacity = min(tok_count, 5 * tok_count * top_count // (4 * n_data))
    routed = tok_count * top_count
    group_rows = n_data * capacity
    slot_count = n_data * capacity
    flat_ids = expert_ids.reshape(routed)
    expert_hot = (flat_ids[:, None] == jnp.arange(n_data, dtype=jnp.int32)[None, :]).astype(
        jnp.int32
    )
    earlier = jnp.sum((jnp.cumsum(expert_hot, axis=0) - expert_hot) * expert_hot, axis=1)
    target = flat_ids * capacity + earlier
    placing = (jnp.arange(slot_count, dtype=jnp.int32)[:, None] == target[None, :]).astype(
        jnp.bfloat16
    )
    token_place = jnp.sum(
        placing.reshape(slot_count, tok_count, top_count).astype(jnp.float32), axis=2
    ).astype(jnp.bfloat16)
    score_total = jnp.sum(scores, axis=1, keepdims=True)
    route_weights = ROUTE_SCALE * scores / score_total
    routed_grad = (route_weights[:, :, None] * out_grad.astype(jnp.float32)[:, None, :]).astype(
        jnp.bfloat16
    )
    routed_grad = routed_grad.reshape(routed, slab_width)
    token_send = jnp.dot(token_place, tokens, preferred_element_type=jnp.float32).astype(
        jnp.bfloat16
    )
    grad_send = jnp.dot(placing, routed_grad, preferred_element_type=jnp.float32).astype(
        jnp.bfloat16
    )
    token_slab, grad_slab = (
        lax.all_to_all(
            token_send.reshape(n_data, capacity, slab_width),
            "dp",
            split_axis=0,
            concat_axis=0,
            tiled=True,
        ),
        lax.all_to_all(
            grad_send.reshape(n_data, capacity, slab_width),
            "dp",
            split_axis=0,
            concat_axis=0,
            tiled=True,
        ),
    )
    token_slab = token_slab.reshape(group_rows, slab_width)
    grad_slab = grad_slab.reshape(group_rows, slab_width)
    in_slab = weight_in[0]
    out_slab = weight_out[0]
    gate_up_own = lax.psum_scatter(
        jnp.dot(token_slab, in_slab, preferred_element_type=jnp.float32),
        "expert",
        scatter_dimension=0,
        tiled=True,
    )
    gate_own, up_own, sig_own = gate_terms(gate_up_own, hidden_units)
    hidden_own = (gate_own * sig_own * up_own).astype(jnp.bfloat16)
    piece = lax.all_gather(hidden_own, "expert", axis=0, tiled=True)
    product = jnp.dot(piece, out_slab, preferred_element_type=jnp.float32)
    out_rows = product
    weight_sum = jnp.einsum("rf,rd->fd", piece, grad_slab, preferred_element_type=jnp.float32)
    out_rows, out_weight_sum = (out_rows, weight_sum)
    expert_out = out_rows.astype(jnp.bfloat16)
    out_blocks = expert_out.reshape(n_data, capacity, slab_width)
    out_back = lax.all_to_all(out_blocks, "dp", split_axis=0, concat_axis=0, tiled=True)
    hidden_grad = lax.psum_scatter(
        jnp.einsum("rd,fd->rf", grad_slab, out_slab, preferred_element_type=jnp.float32),
        "expert",
        scatter_dimension=0,
        tiled=True,
    )
    gate_up_grad = gate_backward(hidden_grad, gate_own, up_own, sig_own)
    piece = lax.all_gather(gate_up_grad, "expert", axis=0, tiled=True)
    product = jnp.einsum("rh,dh->rd", piece, in_slab, preferred_element_type=jnp.float32)
    input_rows = product
    weight_sum = jnp.einsum("rd,rh->dh", token_slab, piece, preferred_element_type=jnp.float32)
    input_rows, in_weight_sum = (input_rows, weight_sum)
    grad_blocks = input_rows.astype(jnp.bfloat16).reshape(n_data, capacity, slab_width)
    grad_back = lax.all_to_all(grad_blocks, "dp", split_axis=0, concat_axis=0, tiled=True)
    outputs_in = out_back.reshape(slot_count, slab_width)
    grads_in = grad_back.reshape(slot_count, slab_width)
    picked = jnp.einsum("sr,sd->rd", placing, outputs_in, preferred_element_type=jnp.float32)
    picked = picked.reshape(tok_count, top_count, slab_width)
    layer_out = jnp.sum(route_weights[:, :, None] * picked, axis=1).astype(jnp.bfloat16)
    partial_dot = jnp.sum(out_grad.astype(jnp.float32)[:, None, :] * picked, axis=2)
    choice_dot = lax.psum(partial_dot, "expert")
    scores_grad = (
        ROUTE_SCALE * choice_dot - jnp.sum(choice_dot * route_weights, axis=1, keepdims=True)
    ) / score_total
    tokens_grad = jnp.einsum(
        "st,sd->td", token_place, grads_in, preferred_element_type=jnp.float32
    ).astype(jnp.bfloat16)
    return (
        layer_out,
        tokens_grad,
        scores_grad,
        in_weight_sum.astype(jnp.bfloat16)[None],
        out_weight_sum.astype(jnp.bfloat16)[None],
    )


def solution(mesh):
    placed = (
        P("dp", "expert"),
        P("dp", None),
        P("dp", None),
        P("dp", "expert", None),
        P("dp", None, "expert"),
        P("dp", "expert"),
    )
    return jax.shard_map(
        body,
        mesh=mesh,
        in_specs=placed,
        out_specs=(
            P("dp", "expert"),
            P("dp", "expert"),
            P("dp", None),
            P("dp", "expert", None),
            P("dp", None, "expert"),
        ),
        check_vma=False,
    )
```

profile of v0, /device:TPU:33, one launch (start us, length us, event | category | flops | bytes accessed | tf_op | source)
XLA Modules:
  0.0 320.6 jit_solution(14053334672853619055)
XLA Ops:
  7.2 0.0 reduce-scatter.5.cloned.1.call-start
  7.2 0.9 copy.31
  8.2 0.1 eq.62
  8.2 0.1 reshape.105
  8.4 9.0 %reduce-window.6 = s32[32,8,128]{2,1,0:T(8,128)S(1)} reduce-window(s32[32,8,128]{2,1,0:T(8,128)S(1)} %fusion.23, s32[]{:T(128)} %constant.13.clone.1), window={size=1x1x128 pad=0_0x0_0x127_0}, to_apply=%region_1.2 | reduce-window | flops 4161536 | bytes 262148 | tf_op jit(solution)/shard_map/reduce-window
  17.4 0.1 slice.16
  17.5 0.1 copy.33
  17.6 0.1 copy.34
  17.7 0.1 broadcast_add_fusion
  17.9 0.7 reduce_sum.59
  18.6 0.7 multiply_divide_fusion
  19.3 0.1 copy.37
  19.4 0.1 mul.93
  19.5 0.9 convert_element_type.56
  20.4 1.6 fusion.5
  22.1 44.8 %all_to_all.20 = bf16[32,40,512]{2,1,0:T(8,128)(2,1)S(1)} all-to-all(bf16[32,40,512]{2,1,0:T(8,128)(2,1)S(1)} %bitcast.71), channel_id=1, replica_groups=mesh['dp'=32,'expert'=8] {'dp'}, dimensions={0} | all-to-all | bytes 2621440 | tf_op jit(solution)/shard_map/all_to_all | solution.py:63
  66.8 1.1 copy-done.2
  67.9 3.9 %fusion.16 = f32[1280,1024]{1,0:T(8,128)} fusion(bf16[1280,512]{1,0:T(8,128)(2,1)S(1)} %bitcast.64, bf16[1,1024,512]{2,1,0:T(8,128)(2,1)S(1)} %copy-done.11), kind=kOutput, calls=%fused_computation.27 | convolution fusion | flops 1342177280 | bytes 7602176 | tf_op jit(solution)/shard_map/rd,fd->rf/dot_general | solution.py:92
  71.8 0.0 reduce-scatter.5.cloned.1.call-update
  71.9 0.0 reduce-scatter.3.cloned.1.call-start
  71.9 0.1 reduce_sum.61
  72.0 0.5 copy-done.10
  72.5 6.7 %fusion.7 = bf16[1280,128]{1,0:T(8,128)(2,1)S(1)} fusion(s32[128,8]{0,1:T(8,128)S(1)} %multiply_add_fusion), kind=kLoop, calls=%fused_computation.14 | loop fusion | flops 3768320 | bytes 331776 | tf_op jit(solution)/shard_map/reduce_sum | solution.py:40
  79.2 0.5 convolution_convert_fusion.3
  79.7 38.6 %all_to_all.21 = bf16[32,40,512]{2,1,0:T(8,128)(2,1)S(1)} all-to-all(bf16[32,40,512]{2,1,0:T(8,128)(2,1)S(1)} %bitcast.63), channel_id=1, replica_groups=mesh['dp'=32,'expert'=8] {'dp'}, dimensions={0} | all-to-all | bytes 2621440 | tf_op jit(solution)/shard_map/all_to_all | solution.py:56
  118.3 1.1 copy-done.3
  119.4 5.5 %fusion.11 = f32[1280,2048]{1,0:T(8,128)} fusion(bf16[1280,512]{1,0:T(8,128)(2,1)S(1)} %bitcast.66, bf16[1,512,2048]{2,1,0:T(8,128)(2,1)S(1)} %copy-done), kind=kOutput, calls=%fused_computation.19 | convolution fusion | flops 2684354560 | bytes 13893632 | tf_op jit(solution)/shard_map/dot_general | solution.py:76
  124.9 0.0 all-gather.3.cloned.1.call-start
  125.0 0.0 reduce-scatter.5.cloned.1.call-done
  125.0 62.0 %reduce-scatter.3.cloned.1.call-done = f32[160,2048]{1,0:T(8,128)} async-done(((f32[1280,2048]{1,0:T(8,128)}), f32[160,2048]{1,0:T(8,128)}) %reduce-scatter.3.cloned.1.call-update) | async-done | bytes 1310736 | tf_op jit(solution)/shard_map/reduce_scatter | solution.py:75
  187.0 2.7 multiply_convert_fusion.1
  189.7 0.0 all-gather.5.cloned.1.call-start
  189.7 0.9 pad_maximum_fusion
  190.6 28.3 %all-gather.3.cloned.1.call-done = bf16[1280,1024]{1,0:T(8,128)(2,1)} async-done(((bf16[160,1024]{1,0:T(8,128)(2,1)}), bf16[1280,1024]{1,0:T(8,128)(2,1)}) %all-gather.3.cloned.1.call-update) | async-done | bytes 2621456 | tf_op jit(solution)/shard_map/all_gather | solution.py:83
  219.0 4.6 %convolution_convert_fusion.2 = bf16[1280,512]{1,0:T(8,128)(2,1)} fusion(bf16[1280,1024]{1,0:T(8,128)(2,1)} %all-gather.3.cloned.1.call-done, bf16[1,1024,512]{2,1,0:T(8,128)(2,1)} %param.10), kind=kOutput, calls=%fused_computation.11 | convolution fusion | flops 1342832640 | bytes 4980736 | tf_op jit(solution)/shard_map/dot_general | solution.py:84
  223.6 9.5 %all-to-all-start.1 = ((bf16[32,40,512]{2,1,0:T(8,128)(2,1)}), bf16[32,40,512]{2,1,0:T(8,128)(2,1)S(1)}, u32[]{:S(2)}, u32[]{:S(2)}) async-start(bf16[32,40,512]{2,1,0:T(8,128)(2,1)} %bitcast.70), calls=%async_computation.2 | async-start | bytes 2621440 | tf_op jit(solution)/shard_map/all_to_all | solution.py:90
  233.1 27.7 %all-gather.5.cloned.1.call-done = bf16[1280,2048]{1,0:T(8,128)(2,1)} async-done(((bf16[160,2048]{1,0:T(8,128)(2,1)}), bf16[1280,2048]{1,0:T(8,128)(2,1)}) %all-gather.5.cloned.1.call-update) | async-done | bytes 5242896 | tf_op jit(solution)/shard_map/all_gather | solution.py:98
  260.8 6.6 %convolution_convert_fusion.1 = bf16[1280,512]{1,0:T(8,128)(2,1)} fusion(bf16[1280,2048]{1,0:T(8,128)(2,1)} %all-gather.5.cloned.1.call-done, bf16[1,512,2048]{2,1,0:T(8,128)(2,1)S(1)} %copy-done), kind=kOutput, calls=%fused_computation.10 | convolution fusion | flops 2685009920 | bytes 8650752 | tf_op jit(solution)/shard_map/rh,dh->rd/dot_general | solution.py:99
  267.4 1.1 copy-done.4
  268.5 9.5 %all-to-all-start.3 = ((bf16[32,40,512]{2,1,0:T(8,128)(2,1)}), bf16[32,40,512]{2,1,0:T(8,128)(2,1)S(1)}, u32[]{:S(2)}, u32[]{:S(2)}) async-start(bf16[32,40,512]{2,1,0:T(8,128)(2,1)} %bitcast.68), calls=%async_computation.5 | async-start | bytes 2621440 | tf_op jit(solution)/shard_map/all_to_all | solution.py:104
  277.9 0.8 fusion
  278.8 4.7 %fusion.13 = bf16[1,1024,512]{2,1,0:T(8,128)(2,1)} fusion(bf16[1280,1024]{1,0:T(8,128)(2,1)} %all-gather.3.cloned.1.call-done, bf16[1280,512]{1,0:T(8,128)(2,1)} %bitcast.65), kind=kOutput, calls=%fused_computation.24 | convolution fusion | flops 1342701568 | bytes 4980736 | tf_op jit(solution)/shard_map/rf,rd->fd/dot_general | solution.py:86
  283.5 2.3 multiply_reduce_fusion
  285.8 12.9 %psum.7 = f32[128,8]{0,1:T(8,128)S(1)} all-reduce(f32[128,8]{0,1:T(8,128)S(1)} %get-tuple-element.5), channel_id=1, replica_groups=mesh['dp'=32,'expert'=8] {'expert'}, use_global_device_ids=true, to_apply=%region_9.10 | all-reduce | flops 1024 | bytes 8192 | tf_op jit(solution)/shard_map/psum | solution.py:111
  298.7 0.6 subtract_divide_fusion
  299.3 7.1 %fusion.6 = bf16[1,512,2048]{2,1,0:T(8,128)(2,1)} fusion(bf16[1280,512]{1,0:T(8,128)(2,1)} %bitcast.67, bf16[1280,2048]{1,0:T(8,128)(2,1)} %all-gather.5.cloned.1.call-done), kind=kOutput, calls=%fused_computation.13 | convolution fusion | flops 2685403136 | bytes 8650752 | tf_op jit(solution)/shard_map/rd,rh->dh/dot_general | solution.py:101
  306.5 5.6 %all-to-all-done.3 = bf16[32,40,512]{2,1,0:T(8,128)(2,1)S(1)} async-done(((bf16[32,40,512]{2,1,0:T(8,128)(2,1)}), bf16[32,40,512]{2,1,0:T(8,128)(2,1)S(1)}, u32[]{:S(2)}, u32[]{:S(2)}) %all-to-all-start.3) | async-done | bytes 1310752 | tf_op jit(solution)/shard_map/all_to_all | solution.py:104
  312.0 2.0 convolution_convert_fusion.5
  (32 shorter events, 0.3 us)
Async XLA Ops:
  7.2 112.2 %copy-start = (bf16[1,512,2048]{2,1,0:T(8,128)(2,1)S(1)}, bf16[1,512,2048]{2,1,0:T(8,128)(2,1)}, u32[]{:S(2)}) copy-start(bf16[1,512,2048]{2,1,0:T(8,128)(2,1)} %param.9) | copy-start | bytes 6291460
  7.2 117.8 %reduce-scatter.5.cloned.1.call-start = ((), (), s32[]{:S(2)}) async-start(), calls=%async_computation.8 | async-start | bytes 5898240 | tf_op jit(solution)/shard_map/reduce_scatter | solution.py:91
  20.4 1.6 copy-start.6
  22.0 45.8 %copy-start.11 = (bf16[1,1024,512]{2,1,0:T(8,128)(2,1)S(1)}, bf16[1,1024,512]{2,1,0:T(8,128)(2,1)}, u32[]{:S(2)}) copy-start(bf16[1,1024,512]{2,1,0:T(8,128)(2,1)} %param.10) | copy-start | bytes 3145732
  66.8 1.1 copy-start.2
  71.8 0.7 copy-start.10
  71.8 7.4 %copy-start.8 = (bf16[128,512]{1,0:T(8,128)(2,1)S(1)}, bf16[128,512]{1,0:T(8,128)(2,1)}, u32[]{:S(2)}) copy-start(bf16[128,512]{1,0:T(8,128)(2,1)} %param.6) | copy-start | bytes 393220
  71.9 115.1 %reduce-scatter.3.cloned.1.call-start = ((), (), s32[]{:S(2)}) async-start(), calls=%async_computation.6 | async-start | bytes 11796480 | tf_op jit(solution)/shard_map/reduce_scatter | solution.py:75
  79.2 39.1 %copy-start.1 = (bf16[1280,128]{1,0:T(8,128)(2,1)}, bf16[1280,128]{1,0:T(8,128)(2,1)S(1)}, u32[]{:S(2)}) copy-start(bf16[1280,128]{1,0:T(8,128)(2,1)S(1)} %fusion.7) | copy-start | bytes 983044
  118.3 1.1 copy-start.3
  124.9 94.0 %all-gather.3.cloned.1.call-start = ((), (), s32[]{:S(2)}) async-start(), calls=%async_computation.7 | async-start | bytes 2949120 | tf_op jit(solution)/shard_map/all_gather | solution.py:83
  189.7 71.2 %all-gather.5.cloned.1.call-start = ((), (), s32[]{:S(2)}) async-start(), calls=%async_computation.9 | async-start | bytes 5898240 | tf_op jit(solution)/shard_map/all_gather | solution.py:98
  223.6 43.8 %all-to-all-start.1 = ((bf16[32,40,512]{2,1,0:T(8,128)(2,1)}), bf16[32,40,512]{2,1,0:T(8,128)(2,1)S(1)}, u32[]{:S(2)}, u32[]{:S(2)}) async-start(bf16[32,40,512]{2,1,0:T(8,128)(2,1)} %bitcast.70), calls=%async_computation.2 | async-start | bytes 2621440 | tf_op jit(solution)/shard_map/all_to_all | solution.py:90
  267.4 1.1 copy-start.4
  268.5 43.6 %all-to-all-start.3 = ((bf16[32,40,512]{2,1,0:T(8,128)(2,1)}), bf16[32,40,512]{2,1,0:T(8,128)(2,1)S(1)}, u32[]{:S(2)}, u32[]{:S(2)}) async-start(bf16[32,40,512]{2,1,0:T(8,128)(2,1)} %bitcast.68), calls=%async_computation.5 | async-start | bytes 2621440 | tf_op jit(solution)/shard_map/all_to_all | solution.py:104
  278.8 4.8 %copy-start.5 = (bf16[32,40,512]{2,1,0:T(8,128)(2,1)S(1)}, bf16[32,40,512]{2,1,0:T(8,128)(2,1)}, u32[]{:S(2)}) copy-start(bf16[32,40,512]{2,1,0:T(8,128)(2,1)} %copy-done.4) | copy-start | bytes 3932164
  278.8 4.8 %copy-start.7 = (f32[128,512]{1,0:T(8,128)S(1)}, f32[128,512]{1,0:T(8,128)}, u32[]{:S(2)}) copy-start(f32[128,512]{1,0:T(8,128)} %copy-done.6) | copy-start | bytes 786436
  283.5 15.2 %copy-start.9 = (f32[128,8]{0,1:T(8,128)S(1)}, f32[128,8]{0,1:T(8,128)}, u32[]{:S(2)}) copy-start(f32[128,8]{0,1:T(8,128)} %param.8) | copy-start | bytes 12292
Sparse Core Ops, SparseCore 0:
  72.0 37.5 reduce-scatter.4
  125.0 61.9 reduce-scatter.2
  189.8 29.1 all-gather.2
  221.2 39.5 all-gather.4
where the time goes:
time: 321 us
  waiting for transfers between devices  124 us (39%)
  blocking collectives  96.2 us (30%)
  matrix products  38.9 us (12%)
  other arithmetic  23.2 us (7%)
  starting transfers between devices  19.2 us (6%)
  between operations  14 us (4%)
  local copies, waits for them, and re-layouts  5.43 us (2%)
    reduce_scatter x1, waiting for transfers between devices, body(): lax.psum_scatter(jnp.dot(token_slab, in_slab, preferred_element_type=jnp....  62 us
    all_to_all x1, blocking collectives, body(): lax.all_to_all(grad_send.reshape(n_data, capacity, slab_width), 'dp', spl...  44.8 us
    all_to_all x1, blocking collectives, body(): lax.all_to_all(token_send.reshape(n_data, capacity, slab_width), 'dp', sp...  38.6 us
    all_gather x1, waiting for transfers between devices, body(): piece = lax.all_gather(hidden_own, 'expert', axis=0, tiled=True)  28.3 us
    all_gather x1, waiting for transfers between devices, body(): piece = lax.all_gather(gate_up_grad, 'expert', axis=0, tiled=True)  27.7 us
    psum x1, blocking collectives, body(): choice_dot = lax.psum(partial_dot, 'expert')  12.9 us
    another operation x4, other arithmetic  11.8 us
    all_to_all x1, starting transfers between devices, body(): lax.all_to_all(out_blocks, 'dp', split_axis=0, concat_axis=0, tiled=True)  9.53 us
  transfers between devices with their start and end apart: 6, of which 4 were waited for; matrix products, arithmetic and copies ran while one was open for 13% of the time, Pallas kernels for 0%

commit v1 on v0

--- a/solution.py
+++ b/solution.py
@@ -80,7 +80,9 @@
     )
     gate_own, up_own, sig_own = gate_terms(gate_up_own, hidden_units)
     hidden_own = (gate_own * sig_own * up_own).astype(jnp.bfloat16)
-    piece = lax.all_gather(hidden_own, "expert", axis=0, tiled=True)
+    piece = jnp.concatenate(
+        lax.all_to_all(jnp.stack([hidden_own] * lax.axis_size("expert")), "expert", 0, 0), axis=0
+    )
     product = jnp.dot(piece, out_slab, preferred_element_type=jnp.float32)
     out_rows = product
     weight_sum = jnp.einsum("rf,rd->fd", piece, grad_slab, preferred_element_type=jnp.float32)

time: 321 us -> 341 us (1.062)
  blocking collectives: 96.2 us -> 152 us
  waiting for transfers between devices: 124 us -> 89.1 us
    all_to_all x0 -> x1, blocking collectives: none -> 54.9 us  [body(): lax.all_to_all(jnp.stack([hidden_own] * lax.axis_size('expert')), 'expert...]
    all_gather x1 -> x0, waiting for transfers between devices: 28.3 us -> none  [body(): piece = lax.all_gather(hidden_own, 'expert', axis=0, tiled=True)]
    all_gather x1, waiting for transfers between devices: 27.7 us -> 0.02 us  [body(): piece = lax.all_gather(gate_up_grad, 'expert', axis=0, tiled=True)]
    all_to_all x1, waiting for transfers between devices: 0.01 us -> 24.8 us  [body(): lax.all_to_all(out_blocks, 'dp', split_axis=0, concat_axis=0, tiled=True)]
  transfers between devices with their start and end apart: 6 -> 5, of which waited for: 4 -> 3; matrix products, arithmetic and copies ran while one was open for 13% -> 11% of each run, Pallas kernels for 0% -> 0%
where the time goes in v1:
time: 341 us; the launch traced here: 337 us
  blocking collectives  152 us (45%)
  waiting for transfers between devices  89.1 us (26%)
  matrix products  36.9 us (11%)
  other arithmetic  22.4 us (7%)
  starting transfers between devices  16.9 us (5%)
  between operations  14 us (4%)
  local copies, waits for them, and re-layouts  5.76 us (2%)
    reduce_scatter x1, waiting for transfers between devices, body(): lax.psum_scatter(jnp.dot(token_slab, in_slab, preferred_element_type=jnp....  62 us
    all_to_all x1, blocking collectives, body(): lax.all_to_all(jnp.stack([hidden_own] * lax.axis_size('expert')), 'expert...  54.9 us
    all_to_all x1, blocking collectives, body(): lax.all_to_all(grad_send.reshape(n_data, capacity, slab_width), 'dp', spl...  44.8 us
    all_to_all x1, blocking collectives, body(): lax.all_to_all(token_send.reshape(n_data, capacity, slab_width), 'dp', sp...  38.6 us
    all_to_all x1, waiting for transfers between devices, body(): lax.all_to_all(out_blocks, 'dp', split_axis=0, concat_axis=0, tiled=True)  24.8 us
    psum x1, blocking collectives, body(): choice_dot = lax.psum(partial_dot, 'expert')  13.9 us
    another operation x4, other arithmetic  11.1 us
    all_to_all x1, starting transfers between devices, body(): lax.all_to_all(out_blocks, 'dp', split_axis=0, concat_axis=0, tiled=True)  9.5 us
  transfers between devices with their start and end apart: 5, of which 3 were waited for; matrix products, arithmetic and copies ran while one was open for 11% of the time, Pallas kernels for 0%

profile of v1, /device:TPU:33, one launch (start us, length us, event | category | flops | bytes accessed | tf_op | source)
XLA Modules:
  0.0 337.2 jit_solution(7834558228390054777)
XLA Ops:
  7.2 0.0 reduce-scatter.5.cloned.1.call-start
  7.2 0.9 copy.31
  8.2 0.1 eq.62
  8.2 0.1 reshape.110
  8.4 9.0 %reduce-window.6 = s32[32,8,128]{2,1,0:T(8,128)S(1)} reduce-window(s32[32,8,128]{2,1,0:T(8,128)S(1)} %fusion.23, s32[]{:T(128)} %constant.13.clone.1), window={size=1x1x128 pad=0_0x0_0x127_0}, to_apply=%region_1.2 | reduce-window | flops 4161536 | bytes 262148 | tf_op jit(solution)/shard_map/reduce-window
  17.4 0.1 slice.16
  17.5 0.1 copy.33
  17.6 0.1 copy.34
  17.7 0.1 broadcast_add_fusion
  17.9 0.7 reduce_sum.59
  18.6 0.7 multiply_divide_fusion
  19.3 0.1 copy.37
  19.4 0.1 mul.93
  19.5 0.9 convert_element_type.56
  20.4 1.6 fusion.5
  22.1 44.8 %all_to_all.25 = bf16[32,40,512]{2,1,0:T(8,128)(2,1)S(1)} all-to-all(bf16[32,40,512]{2,1,0:T(8,128)(2,1)S(1)} %bitcast.74), channel_id=1, replica_groups=mesh['dp'=32,'expert'=8] {'dp'}, dimensions={0} | all-to-all | bytes 2621440 | tf_op jit(solution)/shard_map/all_to_all | solution.py:63
  66.8 1.1 copy-done.3
  67.9 3.9 %fusion.16 = f32[1280,1024]{1,0:T(8,128)} fusion(bf16[1280,512]{1,0:T(8,128)(2,1)S(1)} %bitcast.67, bf16[1,1024,512]{2,1,0:T(8,128)(2,1)S(1)} %copy-done.12), kind=kOutput, calls=%fused_computation.27 | convolution fusion | flops 1342177280 | bytes 7602176 | tf_op jit(solution)/shard_map/rd,fd->rf/dot_general | solution.py:94
  71.8 0.0 reduce-scatter.3.cloned.1.call-start
  71.9 0.1 reduce_sum.61
  72.0 0.5 copy-done.11
  72.5 6.7 %fusion.7 = bf16[1280,128]{1,0:T(8,128)(2,1)S(1)} fusion(s32[128,8]{0,1:T(8,128)S(1)} %multiply_add_fusion), kind=kLoop, calls=%fused_computation.14 | loop fusion | flops 3768320 | bytes 331776 | tf_op jit(solution)/shard_map/reduce_sum | solution.py:40
  79.2 0.5 convolution_convert_fusion.3
  79.7 38.6 %all_to_all.26 = bf16[32,40,512]{2,1,0:T(8,128)(2,1)S(1)} all-to-all(bf16[32,40,512]{2,1,0:T(8,128)(2,1)S(1)} %bitcast.64), channel_id=1, replica_groups=mesh['dp'=32,'expert'=8] {'dp'}, dimensions={0} | all-to-all | bytes 2621440 | tf_op jit(solution)/shard_map/all_to_all | solution.py:56
  118.3 1.1 copy-done.4
  119.4 5.5 %fusion.11 = f32[1280,2048]{1,0:T(8,128)} fusion(bf16[1280,512]{1,0:T(8,128)(2,1)S(1)} %bitcast.69, bf16[1,512,2048]{2,1,0:T(8,128)(2,1)S(1)} %copy-done), kind=kOutput, calls=%fused_computation.19 | convolution fusion | flops 2684354560 | bytes 13893632 | tf_op jit(solution)/shard_map/dot_general | solution.py:76
  124.9 0.0 all-gather.2.cloned.1.call-start
  125.0 0.0 reduce-scatter.5.cloned.1.call-done
  125.0 62.0 %reduce-scatter.3.cloned.1.call-done = f32[160,2048]{1,0:T(8,128)} async-done(((f32[1280,2048]{1,0:T(8,128)}), f32[160,2048]{1,0:T(8,128)}) %reduce-scatter.3.cloned.1.call-update) | async-done | bytes 1310736 | tf_op jit(solution)/shard_map/reduce_scatter | solution.py:75
  187.0 1.9 multiply_convert_fusion.1
  188.9 0.9 pad_maximum_fusion
  189.8 0.3 stack.2
  190.2 54.9 %all_to_all.27 = bf16[8,160,1024]{2,1,0:T(8,128)(2,1)S(1)} all-to-all(bf16[8,160,1024]{2,1,0:T(8,128)(2,1)S(1)} %stack.2), channel_id=1, replica_groups=mesh['dp'=32,'expert'=8] {'expert'}, dimensions={0} | all-to-all | bytes 5242880 | tf_op jit(solution)/shard_map/all_to_all | solution.py:84
  245.1 2.6 convolution_convert_fusion.2
  247.7 9.5 %all-to-all-start.2 = ((bf16[32,40,512]{2,1,0:T(8,128)(2,1)}), bf16[32,40,512]{2,1,0:T(8,128)(2,1)S(1)}, u32[]{:S(2)}, u32[]{:S(2)}) async-start(bf16[32,40,512]{2,1,0:T(8,128)(2,1)} %bitcast.73), calls=%async_computation.3 | async-start | bytes 2621440 | tf_op jit(solution)/shard_map/all_to_all | solution.py:92
  257.2 0.0 all-gather.2.cloned.1.call-done
  257.2 6.6 %convolution_convert_fusion.1 = bf16[1280,512]{1,0:T(8,128)(2,1)} fusion(bf16[1280,2048]{1,0:T(8,128)(2,1)} %all-gather.2.cloned.1.call-done, bf16[1,512,2048]{2,1,0:T(8,128)(2,1)S(1)} %copy-done), kind=kOutput, calls=%fused_computation.10 | convolution fusion | flops 2685009920 | bytes 8650752 | tf_op jit(solution)/shard_map/rh,dh->rd/dot_general | solution.py:101
  263.8 24.8 %all-to-all-done.2 = bf16[32,40,512]{2,1,0:T(8,128)(2,1)S(1)} async-done(((bf16[32,40,512]{2,1,0:T(8,128)(2,1)}), bf16[32,40,512]{2,1,0:T(8,128)(2,1)S(1)}, u32[]{:S(2)}, u32[]{:S(2)}) %all-to-all-start.2) | async-done | bytes 1310752 | tf_op jit(solution)/shard_map/all_to_all | solution.py:92
  288.5 1.1 copy-done.5
  289.6 7.3 %all-to-all-start.4 = ((bf16[32,40,512]{2,1,0:T(8,128)(2,1)}), bf16[32,40,512]{2,1,0:T(8,128)(2,1)S(1)}, u32[]{:S(2)}, u32[]{:S(2)}) async-start(bf16[32,40,512]{2,1,0:T(8,128)(2,1)} %bitcast.71), calls=%async_computation.6 | async-start | bytes 2621440 | tf_op jit(solution)/shard_map/all_to_all | solution.py:106
  296.9 0.8 fusion
  297.7 4.7 %fusion.13 = bf16[1,1024,512]{2,1,0:T(8,128)(2,1)} fusion(bf16[1280,1024]{1,0:T(8,128)(2,1)} %bitcast.66, bf16[1280,512]{1,0:T(8,128)(2,1)} %bitcast.68), kind=kOutput, calls=%fused_computation.24 | convolution fusion | flops 1342701568 | bytes 4980736 | tf_op jit(solution)/shard_map/rf,rd->fd/dot_general | solution.py:88
  302.5 2.3 multiply_reduce_fusion
  304.8 13.9 %psum.7 = f32[128,8]{0,1:T(8,128)S(1)} all-reduce(f32[128,8]{0,1:T(8,128)S(1)} %get-tuple-element.5), channel_id=1, replica_groups=mesh['dp'=32,'expert'=8] {'expert'}, use_global_device_ids=true, to_apply=%region_9.10 | all-reduce | flops 1024 | bytes 8192 | tf_op jit(solution)/shard_map/psum | solution.py:113
  318.7 0.6 subtract_divide_fusion
  319.3 7.1 %fusion.6 = bf16[1,512,2048]{2,1,0:T(8,128)(2,1)} fusion(bf16[1280,512]{1,0:T(8,128)(2,1)} %bitcast.70, bf16[1280,2048]{1,0:T(8,128)(2,1)} %all-gather.2.cloned.1.call-done), kind=kOutput, calls=%fused_computation.13 | convolution fusion | flops 2685403136 | bytes 8650752 | tf_op jit(solution)/shard_map/rd,rh->dh/dot_general | solution.py:103
  326.5 2.2 all-to-all-done.4
  328.7 2.0 convolution_convert_fusion.5
  (35 shorter events, 0.3 us)
Async XLA Ops:
  7.2 112.2 %copy-start = (bf16[1,512,2048]{2,1,0:T(8,128)(2,1)S(1)}, bf16[1,512,2048]{2,1,0:T(8,128)(2,1)}, u32[]{:S(2)}) copy-start(bf16[1,512,2048]{2,1,0:T(8,128)(2,1)} %param.9) | copy-start | bytes 6291460
  7.2 117.8 %reduce-scatter.5.cloned.1.call-start = ((), (), s32[]{:S(2)}) async-start(), calls=%async_computation.8 | async-start | bytes 5898240 | tf_op jit(solution)/shard_map/reduce_scatter | solution.py:93
  20.4 1.6 copy-start.7
  22.0 45.8 %copy-start.12 = (bf16[1,1024,512]{2,1,0:T(8,128)(2,1)S(1)}, bf16[1,1024,512]{2,1,0:T(8,128)(2,1)}, u32[]{:S(2)}) copy-start(bf16[1,1024,512]{2,1,0:T(8,128)(2,1)} %param.10) | copy-start | bytes 3145732
  66.8 1.1 copy-start.3
  71.8 0.7 copy-start.11
  71.8 7.4 %copy-start.9 = (bf16[128,512]{1,0:T(8,128)(2,1)S(1)}, bf16[128,512]{1,0:T(8,128)(2,1)}, u32[]{:S(2)}) copy-start(bf16[128,512]{1,0:T(8,128)(2,1)} %param.6) | copy-start | bytes 393220
  71.8 115.1 %reduce-scatter.3.cloned.1.call-start = ((), (), s32[]{:S(2)}) async-start(), calls=%async_computation.7 | async-start | bytes 11796480 | tf_op jit(solution)/shard_map/reduce_scatter | solution.py:75
  79.2 39.1 %copy-start.1 = (bf16[1280,128]{1,0:T(8,128)(2,1)}, bf16[1280,128]{1,0:T(8,128)(2,1)S(1)}, u32[]{:S(2)}) copy-start(bf16[1280,128]{1,0:T(8,128)(2,1)S(1)} %fusion.7) | copy-start | bytes 983044
  118.3 1.1 copy-start.4
  124.9 132.3 %all-gather.2.cloned.1.call-start = ((), (), s32[]{:S(2)}) async-start(), calls=%async_computation.9 | async-start | bytes 5898240 | tf_op jit(solution)/shard_map/all_gather | solution.py:100
  190.2 54.9 %copy-start.13 = (bf16[1,1024,512]{2,1,0:T(8,128)(2,1)S(1)}, bf16[1,1024,512]{2,1,0:T(8,128)(2,1)}, u32[]{:S(2)}) copy-start(bf16[1,1024,512]{2,1,0:T(8,128)(2,1)} %param.10) | copy-start | bytes 3145732
  245.1 2.6 copy-start.2
  247.7 40.9 %all-to-all-start.2 = ((bf16[32,40,512]{2,1,0:T(8,128)(2,1)}), bf16[32,40,512]{2,1,0:T(8,128)(2,1)S(1)}, u32[]{:S(2)}, u32[]{:S(2)}) async-start(bf16[32,40,512]{2,1,0:T(8,128)(2,1)} %bitcast.73), calls=%async_computation.3 | async-start | bytes 2621440 | tf_op jit(solution)/shard_map/all_to_all | solution.py:92
  288.5 1.1 copy-start.5
  289.6 39.1 %all-to-all-start.4 = ((bf16[32,40,512]{2,1,0:T(8,128)(2,1)}), bf16[32,40,512]{2,1,0:T(8,128)(2,1)S(1)}, u32[]{:S(2)}, u32[]{:S(2)}) async-start(bf16[32,40,512]{2,1,0:T(8,128)(2,1)} %bitcast.71), calls=%async_computation.6 | async-start | bytes 2621440 | tf_op jit(solution)/shard_map/all_to_all | solution.py:106
  297.7 4.8 %copy-start.6 = (bf16[32,40,512]{2,1,0:T(8,128)(2,1)S(1)}, bf16[32,40,512]{2,1,0:T(8,128)(2,1)}, u32[]{:S(2)}) copy-start(bf16[32,40,512]{2,1,0:T(8,128)(2,1)} %copy-done.5) | copy-start | bytes 3932164
  297.7 4.8 %copy-start.8 = (f32[128,512]{1,0:T(8,128)S(1)}, f32[128,512]{1,0:T(8,128)}, u32[]{:S(2)}) copy-start(f32[128,512]{1,0:T(8,128)} %copy-done.7) | copy-start | bytes 786436
  302.5 16.2 %copy-start.10 = (f32[128,8]{0,1:T(8,128)S(1)}, f32[128,8]{0,1:T(8,128)}, u32[]{:S(2)}) copy-start(f32[128,8]{0,1:T(8,128)} %param.8) | copy-start | bytes 12292
Sparse Core Ops, SparseCore 0:
  72.0 37.5 reduce-scatter.4
  125.0 61.9 reduce-scatter.2
  189.9 58.9 all-gather.1
